TPU v7x, 32 devices: a whole 2x2x4 slice. The times are simulated.
32 devices in a mesh: dp: 16 (over z, x, core), head: 2 (over y).
Axes of the slice: x: 2, y: 2, z: 4, core: 2. Of those that a mesh axis runs over, the one named last changes fastest.
Arguments:
- patches: bfloat16 [32, 1024, 768], P('dp'), may hold values from -6 to 6
- keep_mask: int32 [32, 1024], P('dp'), may hold values 0 or 1
- counts: int32 [32], P('dp'), may hold values from 196 to 1024, as said below
- ln_gain: float32 [768], replicated, may hold values from 0.1 to 1.9
- w_in: bfloat16 [2, 768, 2688], P('head'), may hold values from -0.21875 to 0.21875
- q_gain: float32 [12, 64], P('head'), may hold values from 0.1 to 1.9
- k_gain: float32 [12, 64], P('head'), may hold values from 0.1 to 1.9
- w_out: bfloat16 [2, 1920, 768], P('head')
- d_out: bfloat16 [32, 1024, 768], P('dp'), may hold values from -6 to 6
Outputs:
- block_output: bfloat16 [32, 1024, 768], P('dp')
- d_in: bfloat16 [32, 1024, 768], P('dp')
- g_ln: float32 [768], P('dp')
- g_w_in: float32 [2, 768, 2688], P('head', 'dp')
- g_q: float32 [12, 64], P('head', 'dp')
- g_k: float32 [12, 64], P('head', 'dp')
- g_w_out: float32 [2, 1920, 768], P('head', None, 'dp')
Inputs may be any that keep to these rules, and one draw needn't show every extreme that they name: `counts`: each count is 196, 576 or 1024; the first image's is 1024.
All inputs are finite; a program needn't handle non-finite values. No bound on the sum of `keep_mask` on one device may be relied on, other than what follows from the above.
Results may differ from a plain program's by a relative error of at most 0.0091.
Values sent between devices are 32-bit elements; how exact they have to be, the bound alone decides.
A program may use at most 256 MiB of HBM per device.

v0:
```python
import jax
import jax.numpy as jnp
from jax import lax
from jax.sharding import PartitionSpec as P

epsilon = 1e-06


def norm_rows(v):
    centre = v - jnp.mean(v, axis=-1, keepdims=True)
    spread = jnp.mean(centre * centre, axis=-1, keepdims=True)
    return centre * lax.rsqrt(spread + epsilon)


def scaled_norm(values, gain):
    return norm_rows(values) * gain


def exact_gelu(values):
    return jax.nn.gelu(values, approximate=False)


def per_device(patches, keep_mask, counts, ln_gain, w_in, q_gain, k_gain, w_out, d_out):
    seqs, slots, width = patches.shape
    heads, hdim = q_gain.shape
    inner = heads * hdim
    factor = hdim ** (-0.5)
    block = min(512, slots)
    rows = patches.reshape(seqs * slots, width).astype(jnp.float32)
    normed_f, ln_back = jax.vjp(scaled_norm, rows, ln_gain)
    normed = normed_f.astype(jnp.bfloat16)
    proj = jnp.dot(normed, w_in[0], preferred_element_type=jnp.float32)
    q_raw = proj[:, :inner].reshape(-1, heads, hdim)
    k_raw = proj[:, inner : 2 * inner].reshape(-1, heads, hdim)
    q_norm_f, q_back = jax.vjp(scaled_norm, q_raw, q_gain)
    k_norm_f, k_back = jax.vjp(scaled_norm, k_raw, k_gain)
    q_norm = q_norm_f.astype(jnp.bfloat16).reshape(seqs, slots, heads, hdim)
    k_norm = k_norm_f.astype(jnp.bfloat16).reshape(seqs, slots, heads, hdim)
    values = proj[:, 2 * inner : 3 * inner].astype(jnp.bfloat16).reshape(seqs, slots, heads, hdim)
    active, gelu_back = jax.vjp(exact_gelu, proj[:, 3 * inner :])
    hidden = active.astype(jnp.bfloat16)
    slot_ids = jnp.arange(slots, dtype=jnp.int32)
    valid = (slot_ids[None, :] < counts[:, None]) & ((keep_mask == 1) | (slot_ids[None, :] == 0))
    bias = jnp.where(valid, 0.0, -1000000000.0).astype(jnp.float32)

    def forward_one(pack):
        q_seq, k_seq, v_seq, b_seq = pack
        outputs = []
        totals = []
        for start in range(0, slots, block):
            q_blk = q_seq[start : start + block]
            scores = (
                jnp.einsum("qhd,khd->hqk", q_blk, k_seq, preferred_element_type=jnp.float32)
                * factor
            )
            scores = scores + b_seq[None, None, :]
            top = jnp.max(scores, axis=-1, keepdims=True)
            expo = jnp.exp(scores - top)
            summed = jnp.sum(expo, axis=-1, keepdims=True)
            probs = (expo / summed).astype(jnp.bfloat16)
            attn = jnp.einsum("hqk,khd->qhd", probs, v_seq, preferred_element_type=jnp.float32)
            outputs.append(attn.astype(jnp.bfloat16))
            totals.append((top + jnp.log(summed))[..., 0])
        return (jnp.concatenate(outputs, axis=0), jnp.concatenate(totals, axis=1))

    attn_all, log_totals = lax.map(forward_one, (q_norm, k_norm, values, bias))
    joined = jnp.concatenate([attn_all.reshape(-1, inner), hidden], axis=1)
    partial_value = jnp.dot(joined, w_out[0], preferred_element_type=jnp.float32)
    branch = lax.psum(partial_value, "head")
    block_output = (rows + branch).astype(jnp.bfloat16).reshape(patches.shape)
    grad_z = d_out.reshape(-1, width)
    out_term = jnp.einsum("rc,rd->cd", joined, grad_z, preferred_element_type=jnp.float32)[None]
    grad_joined = jnp.einsum("rd,cd->rc", grad_z, w_out[0], preferred_element_type=jnp.float32)
    grad_attn = grad_joined[:, :inner].astype(jnp.bfloat16).reshape(seqs, slots, heads, hdim)
    (grad_u,) = gelu_back(grad_joined[:, inner:])

    def backward_one(pack):
        q_seq, k_seq, v_seq, b_seq, l_seq, g_seq = pack
        key_grad = jnp.zeros((slots, heads, hdim), jnp.float32)
        value_grad = jnp.zeros((slots, heads, hdim), jnp.float32)
        query_parts = []
        for start in range(0, slots, block):
            q_blk = q_seq[start : start + block]
            g_blk = g_seq[start : start + block]
            scores = (
                jnp.einsum("qhd,khd->hqk", q_blk, k_seq, preferred_element_type=jnp.float32)
                * factor
            )
            scores = scores + b_seq[None, None, :]
            probs = jnp.exp(scores - l_seq[:, start : start + block, None])
            grad_p = jnp.einsum("qhd,khd->hqk", g_blk, v_seq, preferred_element_type=jnp.float32)
            inner_sum = jnp.sum(probs * grad_p, axis=-1, keepdims=True)
            grad_s = (probs * (grad_p - inner_sum)).astype(jnp.bfloat16)
            query_parts.append(
                jnp.einsum("hqk,khd->qhd", grad_s, k_seq, preferred_element_type=jnp.float32)
                * factor
            )
            key_grad = (
                key_grad
                + jnp.einsum("hqk,qhd->khd", grad_s, q_blk, preferred_element_type=jnp.float32)
                * factor
            )
            value_grad = value_grad + jnp.einsum(
                "hqk,qhd->khd",
                probs.astype(jnp.bfloat16),
                g_blk,
                preferred_element_type=jnp.float32,
            )
        return (jnp.concatenate(query_parts, axis=0), key_grad, value_grad)

    grad_qn, grad_kn, grad_v = lax.map(
        backward_one, (q_norm, k_norm, values, bias, log_totals, grad_attn)
    )
    grad_q_raw, q_gain_term = q_back(grad_qn.reshape(-1, heads, hdim))
    grad_k_raw, k_gain_term = k_back(grad_kn.reshape(-1, heads, hdim))
    grad_proj = jnp.concatenate(
        [
            grad_q_raw.reshape(-1, inner),
            grad_k_raw.reshape(-1, inner),
            grad_v.reshape(-1, inner),
            grad_u,
        ],
        axis=1,
    ).astype(jnp.bfloat16)
    in_term = jnp.einsum("rc,rg->cg", normed, grad_proj, preferred_element_type=jnp.float32)[None]
    normed_part = jnp.einsum("rg,cg->rc", grad_proj, w_in[0], preferred_element_type=jnp.float32)
    grad_normed = lax.psum(normed_part, "head")
    grad_rows, ln_term = ln_back(grad_normed)
    d_in = (
        (d_out.reshape(-1, width).astype(jnp.float32) + grad_rows)
        .astype(jnp.bfloat16)
        .reshape(patches.shape)
    )
    g_w_in, g_w_out, g_q, g_k, g_ln = (
        lax.psum_scatter(in_term, "dp", scatter_dimension=1, tiled=True),
        lax.psum_scatter(out_term, "dp", scatter_dimension=2, tiled=True),
        lax.psum_scatter(q_gain_term, "dp", scatter_dimension=1, tiled=True),
        lax.psum_scatter(k_gain_term, "dp", scatter_dimension=1, tiled=True),
        lax.psum_scatter(ln_term, "dp", scatter_dimension=0, tiled=True),
    )
    return (block_output, d_in, g_ln, g_w_in, g_q, g_k, g_w_out)


def solution(mesh):
    placed = (
        P("dp", None, None),
        P("dp", None),
        P("dp"),
        P(),
        P("head", None, None),
        P("head", None),
        P("head", None),
        P("head", None, None),
        P("dp", None, None),
    )
    return jax.shard_map(
        per_device,
        mesh=mesh,
        in_specs=placed,
        out_specs=(
            P("dp", None, None),
            P("dp", None, None),
            P("dp"),
            P("head", "dp", None),
            P("head", "dp"),
            P("head", "dp"),
            P("head", None, "dp"),
        ),
        check_vma=False,
    )
```

profile of v0, /device:TPU:0, one launch (start us, length us, event | category | flops | bytes accessed | tf_op | source)
XLA Modules:
  0.0 1182.4 jit_solution(14412227073049610795)
XLA Ops:
  9.0 8.6 fusion.100
  17.6 5.5 copy-done.14
  24.5 11.4 slice.75
  41.1 12.3 %fusion.91 = f32[2048,2688]{1,0:T(8,128)S(1)} fusion(bf16[2048,768]{1,0:T(8,128)(2,1)} %bitcast.323, bf16[1,768,2688]{2,1,0:T(8,128)(2,1)} %param.17), kind=kOutput, calls=%fused_computation.142 | convolution fusion | flops 8455716864 | bytes 29294592 | tf_op jit(solution)/shard_map/dot_general | solution.py:32
  54.8 6.3 copy-done.9
  72.4 5.6 reshape.290
  78.1 3.9 copy.64
  86.7 5.6 reshape.288
  121.0 59.1 %while.26 = (s32[]{:T(128)}, bf16[2,1024,6,64]{1,3,2,0:T(8,128)(2,1)}, f32[2,6,1024]{2,1,0:T(8,128)S(1)}, bf16[2,1024,6,64]{1,3,2,0:T(8,128)(2,1)}, bf16[2,1024,...) while((s32[]{:T(128)}, ...), condition=%wide.region_11.12_spmd, body=%wide.region_6.11_spmd.sunk | while | flops 1688076288 | bytes 107268856 | solution.py:66
  121.1 7.8 fusion.157
  128.9 7.6 fusion.158
  136.5 6.3 fusion.161
  150.6 7.8 fusion.157
  158.4 7.6 fusion.158
  166.1 6.3 fusion.161
  180.1 255.4 %while.27 = (s32[]{:T(128)}, f32[2,1024,6,64]{1,0,3,2:T(2,128)}, f32[2,1024,6,64]{1,0,3,2:T(2,128)}, bf16[2,1024,6,64]{1,3,2,0:T(8,128)(2,1)}, bf16[2,1024,6,64]...) while((s32[]{:T(128)}, f32[2,1024,6,64]{1,0,3,2:T(2,128)}, ...), condition=%wide.region_16.17_spmd, body=%wide.region_13.16_spmd.sunk | while | flops 4122863616 | bytes 368310592 | solution.py:111
  191.2 5.0 bitcast_dynamic-update-slice_fusion.2
  196.1 6.4 fusion.177
  202.5 20.4 %multiply_reduce_fusion.9 = (f32[6,512]{1,0:T(8,128)S(1)}, f32[6,512]{1,0:T(8,128)S(1)}, f32[6,512,1024]{2,1,0:T(8,128)}) fusion(f32[6,512,1024]{2,1,0:T(8,128)} %copy-done.2, f32[6,512]{1,0:T(8,128)S(1)} %get-tuple-element.381, f32[1024]{0:T(1024)S(1)} %bitcast.326, f32[6,512,1024]{2,1,0:T(8,128)} %fusion.177, ...), kind=kOutput, calls=%fused_computation.45.clone.1 | convolution fusion | flops 434104320 | bytes 51565568 | tf_op jit(solution)/shard_map/while/body/eval_jaxpr/qhd,khd->hqk/dot_general | solution.py:91
  222.9 17.4 %multiply_convert_fusion.6 = (bf16[6,512,1024]{2,1,0:T(8,128)(2,1)S(1)}, bf16[6,512,1024]{2,1,0:T(8,128)(2,1)S(1)}) fusion(f32[6,512,1024]{2,1,0:T(8,128)} %get-tuple-element.383, f32[6,512,1024]{2,1,0:T(8,128)} %copy-done.2, f32[6,512]{1,0:T(8,128)S(1)} %get-tuple-element.384, f32[6,512]{1,0:T(8,128)S(1)} %get-tuple-element.381, ...), kind=kLoop, calls=%fused_computation.44.clone.1 | loop fusion | flops 37748736 | bytes 62967808 | tf_op jit(solution)/shard_map/while/body/eval_jaxpr/convert_element_type | solution.py:93
  252.6 27.6 %dynamic_update_slice.29 = f32[2,1024,6,64]{1,0,3,2:T(2,128)} dynamic-update-slice(f32[2,1024,6,64]{1,0,3,2:T(2,128)} %get-tuple-element.432, f32[1,1024,6,64]{1,0,3,2:T(1,128)} %copy.138, s32[]{:T(128)S(6)} %copy.158, s32[]{:T(128)} %constant.61.clone.1..sunk.1, s32[]{:T(128)} %constant.61.clone.1..sunk.1, s32[]{:T(128)} %constant.61.clone.1..sunk.1) | dynamic-update-slice | bytes 3145732 | tf_op jit(solution)/shard_map/while/body/jit(dynamic_update_index_in_dim)/dynamic_update_slice | solution.py:111
  280.2 27.6 %dynamic_update_slice.30 = f32[2,1024,6,64]{1,0,3,2:T(2,128)} dynamic-update-slice(f32[2,1024,6,64]{1,0,3,2:T(2,128)} %get-tuple-element.433, f32[1,1024,6,64]{1,0,3,2:T(1,128)} %copy.139, s32[]{:T(128)S(6)} %copy.158, s32[]{:T(128)} %constant.61.clone.1..sunk.1, s32[]{:T(128)} %constant.61.clone.1..sunk.1, s32[]{:T(128)} %constant.61.clone.1..sunk.1) | dynamic-update-slice | bytes 3145732 | tf_op jit(solution)/shard_map/while/body/jit(dynamic_update_index_in_dim)/dynamic_update_slice | solution.py:111
  318.6 5.0 bitcast_dynamic-update-slice_fusion.2
  323.5 6.4 fusion.177
  329.9 20.4 %multiply_reduce_fusion.9 = (f32[6,512]{1,0:T(8,128)S(1)}, f32[6,512]{1,0:T(8,128)S(1)}, f32[6,512,1024]{2,1,0:T(8,128)}) fusion(f32[6,512,1024]{2,1,0:T(8,128)} %copy-done.2, f32[6,512]{1,0:T(8,128)S(1)} %get-tuple-element.381, f32[1024]{0:T(1024)S(1)} %bitcast.326, f32[6,512,1024]{2,1,0:T(8,128)} %fusion.177, ...), kind=kOutput, calls=%fused_computation.45.clone.1 | convolution fusion | flops 434104320 | bytes 51565568 | tf_op jit(solution)/shard_map/while/body/eval_jaxpr/qhd,khd->hqk/dot_general | solution.py:91
  350.4 17.4 %multiply_convert_fusion.6 = (bf16[6,512,1024]{2,1,0:T(8,128)(2,1)S(1)}, bf16[6,512,1024]{2,1,0:T(8,128)(2,1)S(1)}) fusion(f32[6,512,1024]{2,1,0:T(8,128)} %get-tuple-element.383, f32[6,512,1024]{2,1,0:T(8,128)} %copy-done.2, f32[6,512]{1,0:T(8,128)S(1)} %get-tuple-element.384, f32[6,512]{1,0:T(8,128)S(1)} %get-tuple-element.381, ...), kind=kLoop, calls=%fused_computation.44.clone.1 | loop fusion | flops 37748736 | bytes 62967808 | tf_op jit(solution)/shard_map/while/body/eval_jaxpr/convert_element_type | solution.py:93
  380.0 27.6 %dynamic_update_slice.29 = f32[2,1024,6,64]{1,0,3,2:T(2,128)} dynamic-update-slice(f32[2,1024,6,64]{1,0,3,2:T(2,128)} %get-tuple-element.432, f32[1,1024,6,64]{1,0,3,2:T(1,128)} %copy.138, s32[]{:T(128)S(6)} %copy.158, s32[]{:T(128)} %constant.61.clone.1..sunk.1, s32[]{:T(128)} %constant.61.clone.1..sunk.1, s32[]{:T(128)} %constant.61.clone.1..sunk.1) | dynamic-update-slice | bytes 3145732 | tf_op jit(solution)/shard_map/while/body/jit(dynamic_update_index_in_dim)/dynamic_update_slice | solution.py:111
  407.6 27.6 %dynamic_update_slice.30 = f32[2,1024,6,64]{1,0,3,2:T(2,128)} dynamic-update-slice(f32[2,1024,6,64]{1,0,3,2:T(2,128)} %get-tuple-element.433, f32[1,1024,6,64]{1,0,3,2:T(1,128)} %copy.139, s32[]{:T(128)S(6)} %copy.158, s32[]{:T(128)} %constant.61.clone.1..sunk.1, s32[]{:T(128)} %constant.61.clone.1..sunk.1, s32[]{:T(128)} %constant.61.clone.1..sunk.1) | dynamic-update-slice | bytes 3145732 | tf_op jit(solution)/shard_map/while/body/jit(dynamic_update_index_in_dim)/dynamic_update_slice | solution.py:111
  435.6 5.7 reshape.297
  445.1 5.6 reshape.299
  455.1 12.7 %copy.106 = f32[2048,1536]{1,0:T(8,128)} copy(f32[2048,1536]{0,1:T(8,128)} %slice.75) | data formatting | bytes 25165824
  482.3 5.0 copy.125
  491.0 5.0 copy.123
  517.0 14.2 %multiply_reduce_fusion.2 = (f32[6,64]{1,0:T(8,128)S(1)}, f32[2,1024,6]{1,0,2:T(2,128)S(1)}, f32[2,1024,6]{1,0,2:T(2,128)S(1)}, f32[6,64]{1,0:T(8,128)S(1)}) fusion(f32[2,1024,6,64]{1,0,3,2:T(2,128)} %get-tuple-element.102, f32[2,1024,6,64]{1,0,3,2:T(2,128)} %reshape.290, f32[2,1024,6]{1,0,2:T(2,128)S(1)} %copy-done.37, f32[2,1024,6]{1,0,2:T(2,128)S(1)} %copy-done.33, ...), kind=kLoop, calls=%fused_computation.153 | loop fusion | flops 15703296 | bytes 12982272 | tf_op jit(solution)/shard_map/transpose(jvp())/reduce_sum | solution.py:16
  559.2 31.6 %add_convert_fusion = (bf16[2048,1536]{1,0:T(8,128)(2,1)}, f32[2048,1536]{1,0:T(8,128)S(1)}) fusion(f32[2048,1536]{1,0:T(8,128)} %copy.106, f32[2048,2688]{1,0:T(8,128)} %copy-done.9), kind=kLoop, calls=%fused_computation.95 | loop fusion | flops 226492416 | bytes 44040192 | tf_op jit(solution)/shard_map/convert.4
  590.8 9.9 multiply_convert_fusion.2
  600.7 10.5 fusion.88
  611.3 11.9 %fusion.95 = (bf16[2048,384]{1,0:T(8,128)(2,1)}, bf16[2048,384]{1,0:T(8,128)(2,1)}) fusion(f32[2048,384]{1,0:T(8,128)} %copy.84, f32[2048,384]{1,0:T(8,128)} %copy.82, f32[2048,384]{1,0:T(8,128)} %copy.80, f32[2048,384]{1,0:T(8,128)S(1)} %copy-done.17, f32[2048,384]{1,0:T(8,128)S(1)} %copy-done.16, f32[384]{0:T(512)S(1)} %copy-done.55, ...), kind=kLoop, calls=%fused_computation.146 | loop fusion | flops 12582912 | bytes 40897536 | tf_op jit(solution)/shard_map/convert.1
  623.2 14.6 %fusion.89 = f32[2048,768]{1,0:T(8,128)} fusion(bf16[1,768,2688]{2,1,0:T(8,128)(2,1)} %param.17, bf16[2048,1536]{1,0:T(8,128)(2,1)} %get-tuple-element.225, bf16[2048,384]{1,0:T(8,128)(2,1)S(1)} %copy-done.24, bf16[2048,384]{1,0:T(8,128)(2,1)} %get-tuple-element.238, bf16[2048,384]{1,0:T(8,128)(2,1)} %get-tuple-element.237), kind=kOutput, calls=%fused_computation.140 | convolution fusion | flops 8499757056 | bytes 21430272 | tf_op jit(solution)/shard_map/rg,cg->rc/dot_general | solution.py:126
  638.3 13.0 %fusion.93 = f32[1,1920,768]{2,1,0:T(8,128)} fusion(bf16[2048,768]{1,0:T(8,128)(2,1)} %bitcast.320, bf16[2048,1536]{1,0:T(8,128)(2,1)} %multiply_convert_fusion.2, bf16[2048,384]{1,0:T(8,128)(2,1)} %copy.72), kind=kOutput, calls=%fused_computation.144 | convolution fusion | flops 6055526400 | bytes 16908288 | tf_op jit(solution)/shard_map/rc,rd->cd/dot_general | solution.py:72
  651.3 13.0 %copy.100 = f32[1,1920,768]{1,0,2:T(1,128)} copy(f32[1,1920,768]{2,1,0:T(8,128)} %fusion.93) | data formatting | bytes 11796480 | tf_op jit(solution)/shard_map/broadcast_in_dim | solution.py:72
  664.4 265.0 %all-reduce.11.cloned.1.call-done = (f32[2048,768]{1,0:T(8,128)}, f32[2048,768]{1,0:T(8,128)}) async-done(((f32[2048,768]{1,0:T(8,128)}, f32[2048,768]{1,0:T(8,128)}), (f32[2048,768]{1,0:T(8,128)}, f32[2048,768]{1,0:T(8,128)})) %all-reduce.11.cloned.1.call-update) | async-done | bytes 12582928 | tf_op jit(solution)/shard_map/psum | solution.py:69
  929.4 4.7 fusion.85
  939.0 5.8 fusion.81
  944.9 17.6 %convolution_bitcast_fusion = f32[1,768,2688]{2,1,0:T(8,128)} fusion(bf16[2048,768]{1,0:T(8,128)(2,1)} %get-tuple-element.241, bf16[2048,1536]{1,0:T(8,128)(2,1)} %get-tuple-element.225, bf16[2048,384]{1,0:T(8,128)(2,1)} %copy.95, bf16[2048,384]{1,0:T(8,128)(2,1)} %get-tuple-element.238, bf16[2048,384]{1,0:T(8,128)(2,1)} %get-tuple-element.237), kind=kOutput, calls=%fused_computation.133 | convolution fusion | flops 8499757056 | bytes 22413312 | tf_op jit(solution)/shard_map/rc,rg->cg/dot_general | solution.py:125
  965.2 101.2 %all-reduce.9.cloned.1.call-done = f32[1,1920,768]{1,0,2:T(1,128)} async-done(((f32[1,1920,768]{1,0,2:T(1,128)}), f32[1,1920,768]{1,0,2:T(1,128)}) %all-reduce.9.cloned.1.call-update) | async-done | bytes 5898256
  1068.3 63.4 %all-reduce.4 = (f32[768]{0:T(1024)S(1)}, f32[6,64]{0,1:T(8,128)S(1)}, f32[6,64]{0,1:T(8,128)S(1)}) all-reduce(f32[768]{0:T(1024)S(1)} %get-tuple-element.180, f32[6,64]{0,1:T(8,128)S(1)} %copy.97, f32[6,64]{0,1:T(8,128)S(1)} %copy.99), channel_id=2, replica_groups=mesh['dp'=16,'head'=2] {'dp'}, use_global_device_ids=true, to_apply=%region_25.26.clone | all-reduce | flops 1536 | bytes 12288
  1133.5 42.2 %reduce-scatter.2.cloned.1.call-done = f32[1,48,2688]{2,1,0:T(8,128)} async-done(((f32[1,768,2688]{2,1,0:T(8,128)}), f32[1,48,2688]{2,1,0:T(8,128)}) %reduce-scatter.2.cloned.1.call-update) | async-done | bytes 516112 | tf_op jit(solution)/shard_map/reduce_scatter | solution.py:135
  (271 shorter events, 201.5 us)
Async XLA Ops:
  7.2 922.2 %all-reduce.11.cloned.1.call-start = ((), (), s32[]{:S(2)}) async-start(), calls=%async_computation.3 | async-start | bytes 25165824 | tf_op jit(solution)/shard_map/psum | solution.py:69
  24.5 11.4 copy-start.7
  53.4 7.8 copy-start.9
  70.0 12.0 %copy-start.20 = (f32[2048,6]{0,1:T(8,128)}, f32[2048,6]{0,1:T(8,128)S(1)}, u32[]{:S(2)}) copy-start(f32[2048,6]{0,1:T(8,128)S(1)} %broadcast_multiply_fusion) | copy-start | bytes 147460
  70.1 40.0 %copy-start.32 = (f32[2,1024,6]{1,0,2:T(2,128)}, f32[2,1024,6]{1,0,2:T(2,128)S(1)}, u32[]{:S(2)}) copy-start(f32[2,1024,6]{1,0,2:T(2,128)S(1)} %div.96) | copy-start | bytes 147460
  72.4 37.5 %copy-start.28 = (f32[2048,6]{0,1:T(8,128)}, f32[2048,6]{0,1:T(8,128)S(1)}, u32[]{:S(2)}) copy-start(f32[2048,6]{0,1:T(8,128)S(1)} %multiply_reduce_fusion.6) | copy-start | bytes 147460
  82.0 10.3 copy-start.46
  82.0 11.0 copy-start.48
  84.3 13.2 %copy-start.22 = (f32[2048,6]{0,1:T(8,128)}, f32[2048,6]{0,1:T(8,128)S(1)}, u32[]{:S(2)}) copy-start(f32[2048,6]{0,1:T(8,128)S(1)} %broadcast_multiply_fusion.1) | copy-start | bytes 147460
  84.3 31.2 %copy-start.34 = (f32[2,1024,6]{1,0,2:T(2,128)}, f32[2,1024,6]{1,0,2:T(2,128)S(1)}, u32[]{:S(2)}) copy-start(f32[2,1024,6]{1,0,2:T(2,128)S(1)} %div.93) | copy-start | bytes 147460
  86.7 28.7 %copy-start.30 = (f32[2048,6]{0,1:T(8,128)}, f32[2048,6]{0,1:T(8,128)S(1)}, u32[]{:S(2)}) copy-start(f32[2048,6]{0,1:T(8,128)S(1)} %multiply_reduce_fusion.7) | copy-start | bytes 147460
  110.0 9.3 copy-start.40
  113.8 7.1 copy-start.54
  113.8 7.1 copy-start.57
  115.5 5.5 copy-start.42
  121.1 7.8 copy-start.3
  128.9 7.7 copy-start.11
  150.6 7.8 copy-start.3
  158.4 7.7 copy-start.11
  222.9 17.4 %copy-start.5 = (bf16[2,1024,6,64]{1,3,2,0:T(8,128)(2,1)S(1)}, bf16[2,1024,6,64]{1,3,2,0:T(8,128)(2,1)}, u32[]{:S(2)}) copy-start(bf16[2,1024,6,64]{1,3,2,0:T(8,128)(2,1)} %get-tuple-element.448) | copy-start | bytes 4718596 | tf_op jit(solution)/shard_map/while
  350.4 17.4 %copy-start.5 = (bf16[2,1024,6,64]{1,3,2,0:T(8,128)(2,1)S(1)}, bf16[2,1024,6,64]{1,3,2,0:T(8,128)(2,1)}, u32[]{:S(2)}) copy-start(bf16[2,1024,6,64]{1,3,2,0:T(8,128)(2,1)} %get-tuple-element.448) | copy-start | bytes 4718596 | tf_op jit(solution)/shard_map/while
  435.5 5.7 copy-start.23
  435.5 5.7 copy-start.47
  435.6 9.5 copy-start.31
  441.3 9.5 copy-start.21
  441.3 9.5 copy-start.49
  445.1 10.0 copy-start.29
  491.0 8.5 copy-start.43
  511.3 5.6 copy-start.41
  511.3 5.6 copy-start.45
  511.3 5.7 copy-start.33
  511.3 5.7 copy-start.35
  511.3 5.7 copy-start.37
  511.3 5.7 copy-start.39
  511.3 5.7 copy-start.44
  590.8 9.9 copy-start.25
  600.7 10.6 copy-start.15
  600.7 10.6 copy-start.16
  600.7 10.6 copy-start.17
  600.7 10.6 copy-start.55
  600.7 10.6 copy-start.56
  611.3 11.9 %copy-start.24 = (bf16[2048,384]{1,0:T(8,128)(2,1)S(1)}, bf16[2048,384]{1,0:T(8,128)(2,1)}, u32[]{:S(2)}) copy-start(bf16[2048,384]{1,0:T(8,128)(2,1)} %copy.95) | copy-start | bytes 4718596
  637.8 428.7 %all-reduce.9.cloned.1.call-start = ((), (), s32[]{:S(2)}) async-start(), calls=%async_computation.2 | async-start | bytes 11796480
  651.3 13.1 %copy-start.52 = (f32[1,8,2,128]{3,2,1,0:T(2,128)S(1)}, f32[1,8,2,128]{3,2,1,0:T(2,128)}, u32[]{:S(2)}) copy-start(f32[1,8,2,128]{3,2,1,0:T(2,128)} %get-tuple-element.252) | copy-start | bytes 24580
  651.3 278.1 %copy-start.51 = (f32[768]{0:T(1024)S(1)}, f32[768]{0:T(1024)}, u32[]{:S(2)}) copy-start(f32[768]{0:T(1024)} %param.16) | copy-start | bytes 9220
  664.3 269.8 %copy-start.53 = (f32[1,8,2,128]{3,2,1,0:T(2,128)S(1)}, f32[1,8,2,128]{3,2,1,0:T(2,128)}, u32[]{:S(2)}) copy-start(f32[1,8,2,128]{3,2,1,0:T(2,128)} %get-tuple-element.250) | copy-start | bytes 24580
  664.4 511.3 %reduce-scatter.2.cloned.1.call-start = ((), (), s32[]{:S(2)}) async-start(), calls=%async_computation.1 | async-start | bytes 8773632 | tf_op jit(solution)/shard_map/reduce_scatter | solution.py:135
  929.4 6.5 copy-start.13
  (25 other events, 99.1 us)
Sparse Core Ops, SparseCore 0:
  637.9 291.4 all-reduce.10
  933.1 133.3 all-reduce.8
  1071.1 104.4 reduce-scatter.1
where the time goes:
time: 1200 us; the launch traced here: 1180 us
  waiting for transfers between devices  408 us (34%)
  local copies, waits for them, and re-layouts  320 us (27%)
  matrix products  221 us (18%)
  other arithmetic  152 us (13%)
  blocking collectives  63.4 us (5%)
  between operations  16 us (1%)
    psum x1, waiting for transfers between devices, per_device(): branch = lax.psum(partial_value, 'head')  265 us
    dynamic_update_slice x8, local copies, waits for them, and re-layouts, per_device(): lax.map(backward_one, (q_norm, k_norm, values, bias, log_totals, grad_attn))  121 us
    unnamed x4, waiting for transfers between devices  101 us
    unnamed x1, blocking collectives  63.4 us
    dot_general x4, matrix products, backward_one(): jnp.einsum('qhd,khd->hqk', g_blk, v_seq, preferred_element_type=jnp.float32)  53.6 us
    unnamed x110, local copies, waits for them, and re-layouts  46.2 us
    another operation x5, other arithmetic  43.5 us
    reduce_scatter x1, waiting for transfers between devices, per_device(): lax.psum_scatter(in_term, 'dp', scatter_dimension=1, tiled=True)  42.2 us
  transfers between devices with their start and end apart: 3, of which 3 were waited for; matrix products, arithmetic and copies ran while one was open for 5% of the time, Pallas kernels for 0%

commit v1 on v0

v1 whole, which is shorter than its diff:
```python
import functools
import math

import jax
import jax.numpy as jnp
from jax import lax
from jax.experimental import pallas as pl
from jax.experimental.pallas import tpu as pltpu
from jax.sharding import PartitionSpec as P

EPS = 1e-06
LOG2E = 1.4426950408889634
F32 = jnp.float32
BF16 = jnp.bfloat16
NT = (((1,), (1,)), ((), ()))
NN = (((1,), (0,)), ((), ()))


def mm(a, b, dims=NN):
    return lax.dot_general(a, b, dims, preferred_element_type=F32)


def gelu_parts(u):
    x = jnp.abs(u) * (1.0 / math.sqrt(2.0))
    d = 1.0 + 0.3275911 * x
    r = pl.reciprocal(d, approx=True)
    t = r * (2.0 - d * r)
    g = jnp.exp2(u * u * (-0.5 * LOG2E))
    poly = t * (0.254829592 + t * (-0.284496736 + t * (1.421413741 + t * (-1.453152027 + t * 1.061405429))))
    tail = 0.5 * poly * g
    cdf = jnp.where(u >= 0.0, 1.0 - tail, tail)
    return u * cdf, cdf + u * (g * (1.0 / math.sqrt(2.0 * math.pi)))


def head_norm(v, gain, heads, hdim):
    tokens = v.shape[-1]
    v = v.reshape(heads, hdim, tokens)
    centre = v - jnp.mean(v, axis=1, keepdims=True)
    r = lax.rsqrt(jnp.mean(centre * centre, axis=1, keepdims=True) + EPS)
    n = (centre * r).reshape(heads * hdim, tokens)
    return (n * gain).astype(BF16), r


def project_kernel(heads, hdim, x_ref, dz_ref, lng_ref, win_ref, wout_ref, qg_ref, kg_ref,
                   xnt_ref, dzt_ref, qt_ref, kt_ref, vt_ref, dot_ref, rq_ref, rk_ref, hid_ref, du_ref, wt_ref):
    inner = heads * hdim

    @pl.when(pl.program_id(0) == 0)
    def _():
        wt_ref[...] = win_ref[:, : 3 * inner].T

    x = x_ref[...].astype(F32)
    centre = x - jnp.mean(x, axis=-1, keepdims=True)
    r = lax.rsqrt(jnp.mean(centre * centre, axis=-1, keepdims=True) + EPS)
    xn = (centre * r * lng_ref[...]).astype(BF16)
    dz = dz_ref[...]
    xnt_ref[...] = xn.T
    dzt_ref[...] = dz.T
    qkv = mm(wt_ref[...], xn, NT)
    qn, rq = head_norm(qkv[:inner], qg_ref[...], heads, hdim)
    kn, rk = head_norm(qkv[inner : 2 * inner], kg_ref[...], heads, hdim)
    qt_ref[...] = qn
    kt_ref[...] = kn
    rq_ref[...] = rq
    rk_ref[...] = rk
    vt_ref[...] = qkv[2 * inner :].astype(BF16)
    dot_ref[...] = mm(wout_ref[:inner, :], dz, NT).astype(BF16)
    hidden = win_ref.shape[1] - 3 * inner
    step = 512
    for c in range(0, hidden, step):
        u = mm(xn, win_ref[:, 3 * inner + c : 3 * inner + c + step])
        dh = mm(dz, wout_ref[inner + c : inner + c + step, :], NT)
        h, slope = gelu_parts(u)
        hid_ref[:, c : c + step] = h.astype(BF16)
        du_ref[:, c : c + step] = (dh * slope).astype(BF16)


def project(x, dz, lng, win, wout, qg, kg, heads, hdim, tm=256):
    tokens, width = x.shape
    inner = heads * hdim
    gw = win.shape[1]
    hidden = gw - 3 * inner
    row = lambda n: pl.BlockSpec((tm, n), lambda i: (i, 0))
    col = lambda n: pl.BlockSpec((n, tm), lambda i: (0, i))
    whole = lambda a: pl.BlockSpec(a.shape, lambda i: (0,) * a.ndim, pipeline_mode=pl.Buffered(1))
    stat = pl.BlockSpec((heads, 1, tm), lambda i: (0, 0, i))
    sds = jax.ShapeDtypeStruct
    return pl.pallas_call(
        functools.partial(project_kernel, heads, hdim),
        grid=(tokens // tm,),
        in_specs=[row(width), row(width), whole(lng), whole(win), whole(wout), whole(qg), whole(kg)],
        out_specs=[col(width), col(width), col(inner), col(inner), col(inner), col(inner), stat, stat, row(hidden), row(hidden)],
        out_shape=[sds((width, tokens), BF16), sds((width, tokens), BF16)]
        + [sds((inner, tokens), BF16)] * 4
        + [sds((heads, 1, tokens), F32)] * 2
        + [sds((tokens, hidden), BF16)] * 2,
        scratch_shapes=[pltpu.VMEM((3 * inner, width), BF16)],
        compiler_params=pltpu.CompilerParams(vmem_limit_bytes=58 * 1024 * 1024),
        cost_estimate=pl.CostEstimate(
            flops=2 * tokens * width * (gw + wout.shape[0]), bytes_accessed=tokens * (width * 8 + hidden * 4 + inner * 8) + 4 * width * gw, transcendentals=2 * tokens * hidden
        ),
        name="project",
    )(x, dz, lng, win, wout, qg, kg)


def norm_back(dn, gain_col, unit, r):
    a = dn * gain_col
    m1 = jnp.mean(a, axis=0, keepdims=True)
    m2 = jnp.mean(a * unit, axis=0, keepdims=True)
    return r * (a - m1 - unit * m2)


def attend_kernel(hdim, bq, qt_ref, kt_ref, vt_ref, dot_ref, rq_ref, rk_ref, vrow_ref, qg_ref, kg_ref,
                  o_ref, dq_ref, dk_ref, dv_ref, gq_ref, gk_ref, dqt_s, dkt_s, dvt_s, ot_s):
    tokens = qt_ref.shape[1]
    vrow = vrow_ref[0]
    vrow_b = vrow.astype(BF16)
    scale = 0.125 if hdim == 64 else hdim ** (-0.5)
    for h in range(2):
        rows = slice(h * hdim, (h + 1) * hdim)
        kt = kt_ref[rows, :]
        vt = vt_ref[rows, :]
        kn = kt.T
        ktv = kt * vrow_b
        pad = jnp.zeros((16, tokens), BF16)
        sub = lax.broadcasted_iota(jnp.int32, (16, tokens), 0)
        va_sum = jnp.concatenate([vt * vrow_b, jnp.where(sub == 0, jnp.broadcast_to(vrow, (16, tokens)), 0.0).astype(BF16)], axis=0)
        va = jnp.concatenate([vt, jnp.where(sub < 2, 1.0, 0.0).astype(BF16)], axis=0).T
        dkt_s[rows, :] = jnp.zeros((hdim, tokens), F32)
        dvt_s[rows, :] = jnp.zeros((hdim, tokens), F32)

        def block(i, _):
            at = pl.ds(pl.multiple_of(i * bq, bq), bq)
            qb = qt_ref[rows, at]
            dob = dot_ref[rows, at]
            s = mm(kn, qb)
            e = jnp.exp2(s).astype(BF16)
            oa = mm(va_sum, e)
            linv = 1.0 / oa[hdim : hdim + 1, :]
            o = oa[:hdim, :] * linv
            ot_s[rows, at] = o.astype(BF16)
            dof = dob.astype(F32)
            delta = jnp.sum(dof * o, axis=0, keepdims=True) * linv
            hi = delta.astype(BF16)
            lo = (delta - hi.astype(F32)).astype(BF16)
            dos = (dof * linv).astype(BF16)
            sub16 = lax.broadcasted_iota(jnp.int32, (16, bq), 0)
            minus = jnp.where(sub16 == 0, -hi.astype(F32), jnp.where(sub16 == 1, -lo.astype(F32), 0.0)).astype(BF16)
            t = mm(va, jnp.concatenate([dos, minus], axis=0))
            ds = (e.astype(F32) * t).astype(BF16)
            dvt_s[rows, :] += mm(dos, e, NT)
            dkt_s[rows, :] += mm(qb, ds, NT)
            dqt_s[rows, at] = mm(ktv, ds)
            return 0

        lax.fori_loop(0, tokens // bq, block, 0)

    o_ref[...] = ot_s[...].T
    out = []
    for src, raw, r_ref, g_ref, grad_ref, mul, c in (
        (dqt_s, qt_ref, rq_ref, qg_ref, gq_ref, scale, scale * LOG2E),
        (dkt_s, kt_ref, rk_ref, kg_ref, gk_ref, 1.0 / LOG2E, 1.0),
    ):
        both = []
        for h in range(2):
            rows = slice(h * hdim, (h + 1) * hdim)
            g = g_ref[rows, :]
            unit = raw[rows, :].astype(F32) * (1.0 / (g * c))
            dn = src[rows, :] * mul
            if raw is kt_ref:
                dn = dn * vrow
            grad_ref[rows, :] = jnp.sum(dn * unit, axis=1, keepdims=True)
            both.append(norm_back(dn, g, unit, r_ref[h]).astype(BF16))
        out.append(jnp.concatenate(both, axis=0).T)
    dq_ref[...] = out[0]
    dk_ref[...] = out[1]
    dv_ref[...] = (dvt_s[...] * vrow).astype(BF16).T


def attend(qt, kt, vt, dot, rq, rk, vrow, qg, kg, heads, hdim, image, slots, bq=256):
    inner = heads * hdim
    pair = 2 * hdim
    sds = jax.ShapeDtypeStruct
    tcol = pl.BlockSpec((pair, slots), lambda p: (p, image))
    stat = pl.BlockSpec((2, 1, slots), lambda p: (p, 0, image))
    gain = pl.BlockSpec((pair, 1), lambda p: (p, 0))
    row = pl.BlockSpec((slots, pair), lambda p: (0, p))
    return pl.pallas_call(
        functools.partial(attend_kernel, hdim, bq),
        grid=(heads // 2,),
        in_specs=[tcol, tcol, tcol, tcol, stat, stat, pl.BlockSpec((1, 1, slots), lambda p: (image, 0, 0)), gain, gain],
        out_specs=[row, row, row, row, gain, gain],
        out_shape=[sds((slots, inner), BF16)] * 4 + [sds((inner, 1), F32)] * 2,
        scratch_shapes=[pltpu.VMEM((pair, slots), F32)] * 3 + [pltpu.VMEM((pair, slots), BF16)],
        compiler_params=pltpu.CompilerParams(vmem_limit_bytes=58 * 1024 * 1024),
        cost_estimate=pl.CostEstimate(flops=heads * 6 * 8 * slots * slots * hdim, bytes_accessed=16 * slots * inner, transcendentals=heads * slots * slots),
        name="attend",
    )(qt, kt, vt, dot, rq, rk, vrow, qg, kg)


def rows_kernel(transposed, a_ref, b_ref, wa_ref, wb_ref, out_ref):
    if transposed:
        out_ref[...] = mm(a_ref[...], wa_ref[...], NT) + mm(b_ref[...], wb_ref[...], NT)
    else:
        out_ref[...] = mm(a_ref[...], wa_ref[...]) + mm(b_ref[...], wb_ref[...])


def back_rows_kernel(inner, dq_ref, dk_ref, dv_ref, du_ref, w_ref, out_ref):
    out_ref[...] = (
        mm(dq_ref[...], w_ref[:, :inner], NT)
        + mm(dk_ref[...], w_ref[:, inner : 2 * inner], NT)
        + mm(dv_ref[...], w_ref[:, 2 * inner : 3 * inner], NT)
        + mm(du_ref[...], w_ref[:, 3 * inner :], NT)
    )


def back_rows(dq, dk, dv, du, win, image, tm=256):
    slots, inner = dq.shape
    width, gw = win.shape
    hidden = gw - 3 * inner
    steps = slots // tm
    row = pl.BlockSpec((tm, inner), lambda i: (i, 0))
    return pl.pallas_call(
        functools.partial(back_rows_kernel, inner),
        grid=(steps,),
        in_specs=[row, row, row, pl.BlockSpec((tm, hidden), lambda i: (image * steps + i, 0)), pl.BlockSpec(win.shape, lambda i: (0, 0), pipeline_mode=pl.Buffered(1))],
        out_specs=pl.BlockSpec((tm, width), lambda i: (i, 0)),
        out_shape=jax.ShapeDtypeStruct((slots, width), F32),
        compiler_params=pltpu.CompilerParams(vmem_limit_bytes=40 * 1024 * 1024),
        cost_estimate=pl.CostEstimate(flops=2 * slots * width * gw, bytes_accessed=slots * (2 * gw + 4 * width) + 2 * width * gw, transcendentals=0),
        name="back_rows",
    )(dq, dk, dv, du, win)


def out_rows_kernel(inner, o_ref, hid_ref, w_ref, out_ref):
    out_ref[...] = mm(o_ref[...], w_ref[:inner, :]) + mm(hid_ref[...], w_ref[inner:, :])


def out_rows(o, hid, wout, image, tm=256):
    slots, inner = o.shape
    go, width = wout.shape
    steps = slots // tm
    return pl.pallas_call(
        functools.partial(out_rows_kernel, inner),
        grid=(steps,),
        in_specs=[pl.BlockSpec((tm, inner), lambda i: (i, 0)), pl.BlockSpec((tm, go - inner), lambda i: (image * steps + i, 0)), pl.BlockSpec(wout.shape, lambda i: (0, 0), pipeline_mode=pl.Buffered(1))],
        out_specs=pl.BlockSpec((tm, width), lambda i: (i, 0)),
        out_shape=jax.ShapeDtypeStruct((slots, width), F32),
        compiler_params=pltpu.CompilerParams(vmem_limit_bytes=40 * 1024 * 1024),
        cost_estimate=pl.CostEstimate(flops=2 * slots * width * go, bytes_accessed=slots * (2 * go + 4 * width) + 2 * width * go, transcendentals=0),
        name="out_rows",
    )(o, hid, wout)


def per_device(patches, keep_mask, counts, ln_gain, w_in, q_gain, k_gain, w_out, d_out):
    seqs, slots, width = patches.shape
    heads, hdim = q_gain.shape
    inner = heads * hdim
    swap = [(0, 1), (1, 0)]
    scale = hdim ** (-0.5)
    win, wout = w_in[0], w_out[0]
    x = patches.reshape(seqs * slots, width)
    dz = d_out.reshape(seqs * slots, width)
    slot_ids = jnp.arange(slots, dtype=jnp.int32)
    valid = (slot_ids[None, :] < counts[:, None]) & ((keep_mask == 1) | (slot_ids[None, :] == 0))
    vrow = valid.astype(F32).reshape(seqs, 1, slots)
    qg = q_gain.reshape(inner, 1)
    kg = k_gain.reshape(inner, 1)
    xnt, dzt, qt, kt, vt, dot, rq, rk, hid, du = project(x, dz, ln_gain.reshape(1, width), win, wout, qg * (scale * LOG2E), kg, heads, hdim)
    outs, grads_in = [], []
    os, dqs, gqs, gks = [], [], [], []
    for s in range(seqs):
        o, dq, dk, dv, gq, gk = attend(qt, kt, vt, dot, rq, rk, vrow, qg, kg, heads, hdim, s, slots)
        dxn = back_rows(dq, dk, dv, du, win, s)
        grads_in.append((dxn, lax.ppermute(dxn, "head", swap)))
        z = out_rows(o, hid, wout, s)
        outs.append((z, lax.ppermute(z, "head", swap)))
        os.append(o)
        dqs.append(jnp.concatenate([dq, dk, dv], axis=1))
        gqs.append(gq)
        gks.append(gk)
    o = jnp.concatenate(os, axis=0)
    dqkv = jnp.concatenate(dqs, axis=0)
    d = lambda a, b: jnp.dot(a, b, preferred_element_type=F32)
    early = jnp.concatenate([d(dzt, hid), d(xnt, du)], axis=1)
    late = jnp.concatenate([d(dzt, o), d(xnt, dqkv)], axis=1)
    rs = lambda v: lax.psum_scatter(v, "dp", scatter_dimension=0, tiled=True)
    early = rs(early)
    late = rs(late)
    hidden = hid.shape[1]
    g_w_out = jnp.concatenate([late[:, :inner], early[:, :hidden]], axis=1).T[None]
    g_w_in = jnp.concatenate([late[:, inner:], early[:, hidden:]], axis=1)[None]
    block_output = jnp.stack([(patches[s].astype(F32) + outs[s][0] + outs[s][1]).astype(BF16) for s in range(seqs)])
    d_in, ln_term = [], jnp.zeros((width,), F32)
    for s in range(seqs):
        g = grads_in[s][0] + grads_in[s][1]
        xs = patches[s].astype(F32)
        centre = xs - jnp.mean(xs, axis=-1, keepdims=True)
        r = lax.rsqrt(jnp.mean(centre * centre, axis=-1, keepdims=True) + EPS)
        n = centre * r
        a = g * ln_gain
        back = r * (a - jnp.mean(a, axis=-1, keepdims=True) - n * jnp.mean(a * n, axis=-1, keepdims=True))
        d_in.append((d_out[s].astype(F32) + back).astype(BF16))
        ln_term = ln_term + jnp.sum(g * n, axis=0)
    d_in = jnp.stack(d_in)
    g_q = sum(gqs).reshape(heads, hdim)
    g_k = sum(gks).reshape(heads, hdim)
    return (
        block_output,
        d_in,
        rs(ln_term),
        g_w_in,
        lax.psum_scatter(g_q, "dp", scatter_dimension=1, tiled=True),
        lax.psum_scatter(g_k, "dp", scatter_dimension=1, tiled=True),
        g_w_out,
    )


def solution(mesh):
    placed = (
        P("dp", None, None),
        P("dp", None),
        P("dp"),
        P(),
        P("head", None, None),
        P("head", None),
        P("head", None),
        P("head", None, None),
        P("dp", None, None),
    )
    return jax.shard_map(
        per_device,
        mesh=mesh,
        in_specs=placed,
        out_specs=(
            P("dp", None, None),
            P("dp", None, None),
            P("dp"),
            P("head", "dp", None),
            P("head", "dp"),
            P("head", "dp"),
            P("head", None, "dp"),
        ),
        check_vma=False,
    )
```

time: 1200 us -> 466 us (0.39); the launches traced: 1180 us -> 465 us
  local copies, waits for them, and re-layouts: 320 us -> 15.3 us
  waiting for transfers between devices: 408 us -> 178 us
  matrix products: 221 us -> 26.2 us
  Pallas kernels: 0 us -> 125 us
  other arithmetic: 152 us -> 39.5 us
    psum x1 -> x0, waiting for transfers between devices: 265 us -> none  [per_device(): branch = lax.psum(partial_value, 'head')]
    dot_general x34 -> x4, matrix products: 221 us -> 26.2 us  [per_device(): d = lambda a, b: jnp.dot(a, b, preferred_element_type=F32)]
    ppermute x0 -> x4, waiting for transfers between devices: none -> 178 us  [the longest x2 110 us: per_device(): grads_in.append((dxn, lax.ppermute(dxn, 'head', swap)))]
    pallas_call x0 -> x7, Pallas kernels: none -> 125 us  [the longest x2 69.4 us: attend(): pl.pallas_call(functools.partial(attend_kernel, hdim, bq), grid=(heads //...]
    dynamic_update_slice x8 -> x0, local copies, waits for them, and re-layouts: 121 us -> none  [per_device(): lax.map(backward_one, (q_norm, k_norm, values, bias, log_totals, grad_attn))]
    unnamed x4 -> x2, waiting for transfers between devices: 101 us -> 0.03 us
    convert_element_type x7 -> x0, other arithmetic: 60.3 us -> none  [the longest x2 34.7 us: backward_one(): grad_s = (probs * (grad_p - inner_sum)).astype(jnp.bfloat16)]
    reduce_scatter x1 -> x2, waiting for transfers between devices: 42.2 us -> 0.02 us  [per_device(): rs = lambda v: lax.psum_scatter(v, 'dp', scatter_dimension=0, tiled=True)]
  transfers between devices with their start and end apart: 3 -> 6, of which waited for: 3 -> 3; matrix products, arithmetic and copies ran while one was open for 5% -> 12% of each run, Pallas kernels for 0% -> 5%
where the time goes in v1:
time: 466 us; the launch traced here: 465 us
  waiting for transfers between devices  178 us (38%)
  Pallas kernels  125 us (27%)
  blocking collectives  60.1 us (13%)
  other arithmetic  39.5 us (8%)
  matrix products  26.2 us (6%)
  between operations  15.7 us (3%)
  local copies, waits for them, and re-layouts  15.3 us (3%)
  starting transfers between devices  5.44 us (1%)
    ppermute x2, waiting for transfers between devices, per_device(): grads_in.append((dxn, lax.ppermute(dxn, 'head', swap)))  110 us
    pallas_call x2, Pallas kernels, attend(): pl.pallas_call(functools.partial(attend_kernel, hdim, bq), grid=(heads //...  69.4 us
    ppermute x2, waiting for transfers between devices, per_device(): outs.append((z, lax.ppermute(z, 'head', swap)))  67.4 us
    unnamed x1, blocking collectives  60.1 us
    pallas_call x1, Pallas kernels, project(): pl.pallas_call(functools.partial(project_kernel, heads, hdim), grid=(toke...  31.3 us
    dot_general x4, matrix products, per_device(): d = lambda a, b: jnp.dot(a, b, preferred_element_type=F32)  26.2 us
    pallas_call x2, Pallas kernels, back_rows(): pl.pallas_call(functools.partial(back_rows_kernel, inner), grid=(steps,),...  15.4 us
    reduce_sum x1, other arithmetic, per_device(): ln_term = ln_term + jnp.sum(g * n, axis=0)  10.1 us
  transfers between devices with their start and end apart: 6, of which 3 were waited for; matrix products, arithmetic and copies ran while one was open for 12% of the time, Pallas kernels for 5%

profile of v1, /device:TPU:0, one launch (start us, length us, event | category | flops | bytes accessed | tf_op | source)
XLA Modules:
  0.0 464.8 jit_solution(5300526364232398800)
XLA Ops:
  7.2 1.3 reshape.107.lng_ref
  8.5 0.8 and_convert_fusion
  9.3 0.6 reshape.115.vrow_ref
  9.9 0.8 reshape.125.qg_ref
  10.7 1.6 reshape.126.kg_ref
  12.3 0.7 broadcast_multiply_fusion.qg_ref
  13.0 31.3 %project.1 = (bf16[768,2048]{1,0:T(8,128)(2,1)}, bf16[768,2048]{1,0:T(8,128)(2,1)}, bf16[384,2048]{1,0:T(8,128)(2,1)}, bf16[384,2048]{1,0:T(8,128)(2,1)}, bf16[3...) custom-call(bf16[2048,768]{1,0:T(8,128)(2,1)} %bitcast.119, ...), custom_call_target="tpu_custom_call" | custom-call | flops 14495514624 | bytes 39714816 | tf_op jit(solution)/shard_map/project/pallas_call | solution.py:88
  44.3 34.7 %attend.3 = (bf16[1024,384]{1,0:T(8,128)(2,1)}, bf16[1024,384]{1,0:T(8,128)(2,1)}, bf16[1024,384]{1,0:T(8,128)(2,1)}, bf16[1024,384]{1,0:T(8,128)(2,1)}, f32[384,1]{1,0:T(8,128)}, /*index=5*/f32[384,1]{1,0:T(8,128)}) custom-call(bf16[384,2048]{1,0:T(8,128)(2,1)} %get-tuple-element.29.qt_ref, bf16[384,2048]{1,0:T(8,128)(2,1)} %get-tuple-element.30.kt_ref, ...), custom_call_target="tpu_custom_call" | custom-call | flops 19327352832 | bytes 6291456 | tf_op jit(solution)/shard_map/attend/pallas_call | solution.py:188
  79.0 34.7 %attend.2 = (bf16[1024,384]{1,0:T(8,128)(2,1)}, bf16[1024,384]{1,0:T(8,128)(2,1)}, bf16[1024,384]{1,0:T(8,128)(2,1)}, bf16[1024,384]{1,0:T(8,128)(2,1)}, f32[384,1]{1,0:T(8,128)}, /*index=5*/f32[384,1]{1,0:T(8,128)}) custom-call(bf16[384,2048]{1,0:T(8,128)(2,1)} %get-tuple-element.29.qt_ref, bf16[384,2048]{1,0:T(8,128)(2,1)} %get-tuple-element.30.kt_ref, ...), custom_call_target="tpu_custom_call" | custom-call | flops 19327352832 | bytes 6291456 | tf_op jit(solution)/shard_map/attend/pallas_call | solution.py:188
  113.8 4.0 fusion.48
  117.9 0.4 copy-done.21
  118.3 4.2 fusion
  122.5 2.8 pad_maximum_fusion.1
  125.4 8.2 %fusion.55 = f32[768,1536]{1,0:T(8,128)S(1)} fusion(bf16[768,2048]{1,0:T(8,128)(2,1)} %get-tuple-element.45, bf16[2048,1536]{1,0:T(8,128)(2,1)} %get-tuple-element.36.hid_ref), kind=kOutput, calls=%fused_computation.82 | convolution fusion | flops 4831838208 | bytes 14155776 | tf_op jit(solution)/shard_map/dot_general | solution.py:284
  133.7 9.8 %fusion.56 = f32[768,1536]{1,0:T(8,128)} fusion(bf16[768,2048]{1,0:T(8,128)(2,1)S(1)} %copy-done.22, bf16[2048,1536]{1,0:T(8,128)(2,1)} %get-tuple-element.41.du_ref), kind=kOutput, calls=%fused_computation.83 | convolution fusion | flops 4831838208 | bytes 14155776 | tf_op jit(solution)/shard_map/dot_general | solution.py:284
  143.4 7.3 %pad_maximum_fusion = f32[768,3072]{1,0:T(8,128)} fusion(f32[768,1536]{1,0:T(8,128)} %fusion.56, f32[768,1536]{1,0:T(8,128)S(1)} %fusion.55), kind=kLoop, calls=%fused_computation | loop fusion | flops 2359296 | bytes 18874368 | tf_op jit(solution)/shard_map/concatenate | solution.py:285
  150.7 2.2 copy-done
  152.9 1.1 copy-done.8
  154.0 1.1 copy-done.10
  155.2 7.8 %back_rows.2 = f32[1024,768]{1,0:T(8,128)} custom-call(bf16[1024,384]{1,0:T(8,128)(2,1)S(1)} %copy-done.6, bf16[1024,384]{1,0:T(8,128)(2,1)S(1)} %copy-done.8, bf16[1024,384]{1,0:T(8,128)(2,1)S(1)} %copy-done.10, bf16[2048,1536]{1,0:T(8,128)(2,1)} %get-tuple-element.41.du_ref, bf16[768,2688]{1,0:T(8,128)(2,1)S(1)} %bitcast.114), custom_call_target="tpu_custom_call" | custom-call | flops 4227858432 | bytes 12779520 | tf_op jit(solution)/shard_map/back_rows/pallas_call | solution.py:223
  163.0 3.1 collective-permute-start.2
  166.1 7.6 %back_rows.3 = f32[1024,768]{1,0:T(8,128)} custom-call(bf16[1024,384]{1,0:T(8,128)(2,1)S(1)} %copy-done.3, bf16[1024,384]{1,0:T(8,128)(2,1)S(1)} %copy-done.4, bf16[1024,384]{1,0:T(8,128)(2,1)S(1)} %copy-done.5, bf16[2048,1536]{1,0:T(8,128)(2,1)} %get-tuple-element.41.du_ref, bf16[768,2688]{1,0:T(8,128)(2,1)S(1)} %bitcast.115), custom_call_target="tpu_custom_call" | custom-call | flops 4227858432 | bytes 12779520 | tf_op jit(solution)/shard_map/back_rows/pallas_call | solution.py:223
  173.7 0.2 collective-permute-start.3
  173.9 4.9 %out_rows.3 = f32[1024,768]{1,0:T(8,128)} custom-call(bf16[1024,384]{1,0:T(8,128)(2,1)S(1)} %copy-done.12, bf16[2048,1536]{1,0:T(8,128)(2,1)S(1)} %bitcast.112, bf16[1920,768]{1,0:T(8,128)(2,1)S(1)} %bitcast.117), custom_call_target="tpu_custom_call" | custom-call | flops 3019898880 | bytes 10027008 | tf_op jit(solution)/shard_map/out_rows/pallas_call | solution.py:243
  178.8 1.8 collective-permute-start.1
  180.6 3.9 out_rows.2
  184.6 0.2 collective-permute-start
  184.8 0.6 dynamic-slice
  186.7 1.2 add_reduce_fusion
  188.1 2.6 convert_reduce_fusion.1
  190.7 0.4 copy-done.14
  191.1 1.4 fusion.39
  192.5 42.8 %collective-permute-done.2 = f32[1024,768]{1,0:T(8,128)} collective-permute-done((f32[1024,768]{1,0:T(8,128)}, f32[1024,768]{1,0:T(8,128)}, u32[]{:S(2)}, u32[]{:S(2)}) %collective-permute-start.2) | collective-permute-done | bytes 3145760 | tf_op jit(solution)/shard_map/ppermute | solution.py:275
  235.3 67.4 %collective-permute-done.3 = f32[1024,768]{1,0:T(8,128)} collective-permute-done((f32[1024,768]{1,0:T(8,128)}, f32[1024,768]{1,0:T(8,128)}, u32[]{:S(2)}, u32[]{:S(2)}) %collective-permute-start.3) | collective-permute-done | bytes 3145760 | tf_op jit(solution)/shard_map/ppermute | solution.py:275
  302.7 67.4 %collective-permute-done.1 = f32[1024,768]{1,0:T(8,128)} collective-permute-done((f32[1024,768]{1,0:T(8,128)}, f32[1024,768]{1,0:T(8,128)}, u32[]{:S(2)}, u32[]{:S(2)}) %collective-permute-start.1) | collective-permute-done | bytes 3145760 | tf_op jit(solution)/shard_map/ppermute | solution.py:277
  370.1 10.1 %fusion.38 = (f32[768]{0:T(1024)S(1)}, f32[1024]{0:T(1024)S(1)}, f32[1024]{0:T(1024)S(1)}, f32[768]{0:T(1024)S(1)}, f32[1024]{0:T(1024)S(1)}, /*index=5*/f32[102...) fusion(f32[1024]{0:T(1024)S(1)} %add_rsqrt_fusion.1, ...), kind=kLoop, calls=%fused_computation.44 | loop fusion | flops 18082304 | bytes 29926400 | tf_op jit(solution)/shard_map/reduce_sum | solution.py:304
  380.3 60.1 %all-reduce.3 = (f32[768]{0:T(1024)S(1)}, f32[6,64]{1,0:T(8,128)S(1)}, f32[6,64]{1,0:T(8,128)S(1)}) all-reduce(f32[768]{0:T(1024)S(1)} %add.69, f32[6,64]{1,0:T(8,128)S(1)} %reshape.112, f32[6,64]{1,0:T(8,128)S(1)} %reshape.113), channel_id=2, replica_groups=mesh['dp'=16,'head'=2] {'dp'}, use_global_device_ids=true, to_apply=%region_10.0.clone | all-reduce | flops 1536 | bytes 12288
  440.4 0.7 copy.45
  441.2 0.7 copy.46
  441.8 0.6 dynamic-slice.1
  442.4 7.1 %fusion.46 = (bf16[1,1024,768]{2,1,0:T(8,128)(2,1)S(1)}, bf16[1,1024,768]{2,1,0:T(8,128)(2,1)S(1)}, bf16[1,1024,768]{2,1,0:T(8,128)(2,1)S(1)}) fusion(f32[1024,768]{1,0:T(8,128)} %get-tuple-element.87, f32[1024]{0:T(1024)S(1)} %broadcast_multiply_fusion.4, f32[1024]{0:T(1024)S(1)} %broadcast_multiply_fusion.5, f32[768]{0:T(1024)S(1)} %copy-done.19, ...), kind=kLoop, calls=%fused_computation.56 | loop fusion | flops 19660800 | bytes 23628800 | tf_op jit(solution)/shard_map/stack | solution.py:305
  449.5 1.9 pad_maximum_fusion.3
  451.5 1.9 pad_maximum_fusion.2
  453.4 0.9 slice.36
  454.3 0.9 slice.34
  455.3 1.1 fusion.54
  456.4 0.8 maximum_bitcast_fusion.1
  457.1 0.8 maximum_bitcast_fusion
  (66 shorter events, 0.6 us)
Async XLA Ops:
  7.2 446.2 %reduce-scatter.5.cloned.1.call-start = ((), (), s32[]{:S(2)}) async-start(), calls=%async_computation.2 | async-start | bytes 5013504 | tf_op jit(solution)/shard_map/reduce_scatter | solution.py:287
  10.7 33.5 %copy-start.16 = (f32[384,1]{1,0:T(8,128)}, f32[384,1]{1,0:T(8,128)S(1)}, u32[]{:S(2)}) copy-start(f32[384,1]{1,0:T(8,128)S(1)} %reshape.125.qg_ref) | copy-start | bytes 4612
  79.0 34.8 %copy-start.11 = (bf16[1024,384]{1,0:T(8,128)(2,1)S(1)}, bf16[1024,384]{1,0:T(8,128)(2,1)}, u32[]{:S(2)}) copy-start(bf16[1024,384]{1,0:T(8,128)(2,1)} %get-tuple-element.37.o_ref) | copy-start | bytes 2359300
  113.7 4.1 copy-start.3
  113.7 4.1 copy-start.4
  113.8 4.1 copy-start.5
  113.8 4.1 copy-start.6
  113.8 4.1 copy-start.7
  113.8 4.1 copy-start.9
  113.8 4.5 copy-start.21
  125.4 329.9 %reduce-scatter.7.cloned.1.call-start = ((), (), s32[]{:S(2)}) async-start(), calls=%async_computation.3 | async-start | bytes 10027008 | tf_op jit(solution)/shard_map/reduce_scatter | solution.py:287
  125.4 8.2 %copy-start.22 = (bf16[768,2048]{1,0:T(8,128)(2,1)S(1)}, bf16[768,2048]{1,0:T(8,128)(2,1)}, u32[]{:S(2)}) copy-start(bf16[768,2048]{1,0:T(8,128)(2,1)} %get-tuple-element.46) | copy-start | bytes 9437188
  150.7 2.2 copy-start
  152.9 1.1 copy-start.8
  154.0 1.1 copy-start.10
  155.2 18.7 %slice-start = ((s8[6291456]{0:T(1024)(128)(4,1)}), s8[4194304]{0:T(1024)(128)(4,1)S(1)}, s32[]{:S(2)}) async-start(s8[6291456]{0:T(1024)(128)(4,1)} %bitcast.111), calls=%async_computation.4 | async-start | bytes 8388608
  163.0 10.9 %slice-start.1 = ((s8[6291456]{0:T(1024)(128)(4,1)}), s8[2097152]{0:T(1024)(128)(4,1)S(1)}, s32[]{:S(2)}) async-start(s8[6291456]{0:T(1024)(128)(4,1)} %bitcast.111), calls=%async_computation.5 | async-start | bytes 4194304
  163.0 10.9 %copy-start.1 = (bf16[1,1920,768]{2,1,0:T(8,128)(2,1)S(1)}, bf16[1,1920,768]{2,1,0:T(8,128)(2,1)}, u32[]{:S(2)}) copy-start(bf16[1,1920,768]{2,1,0:T(8,128)(2,1)} %param.16) | copy-start | bytes 8847364
  163.0 10.9 %copy-start.12 = (bf16[1024,384]{1,0:T(8,128)(2,1)S(1)}, bf16[1024,384]{1,0:T(8,128)(2,1)}, u32[]{:S(2)}) copy-start(bf16[1024,384]{1,0:T(8,128)(2,1)} %get-tuple-element.37.o_ref) | copy-start | bytes 2359300
  163.0 72.3 %collective-permute-start.2 = (f32[1024,768]{1,0:T(8,128)}, f32[1024,768]{1,0:T(8,128)}, u32[]{:S(2)}, u32[]{:S(2)}) collective-permute-start(f32[1024,768]{1,0:T(8,128)} %back_rows.2), channel_id=1, source_target_pairs={{0,1},{1,0},{2,3},{3,2},{4,5},{5,4},{6,7},{7,6},{8,9},{9,8},{10,11... | collective-permute-start | bytes 9437192 | tf_op jit(solution)/shard_map/ppermute | solution.py:275
  173.7 6.9 %copy-start.2 = (bf16[1,1920,768]{2,1,0:T(8,128)(2,1)S(1)}, bf16[1,1920,768]{2,1,0:T(8,128)(2,1)}, u32[]{:S(2)}) copy-start(bf16[1,1920,768]{2,1,0:T(8,128)(2,1)} %param.16) | copy-start | bytes 8847364
  173.7 6.9 %copy-start.13 = (bf16[1024,384]{1,0:T(8,128)(2,1)S(1)}, bf16[1024,384]{1,0:T(8,128)(2,1)}, u32[]{:S(2)}) copy-start(bf16[1024,384]{1,0:T(8,128)(2,1)} %get-tuple-element.35.o_ref) | copy-start | bytes 2359300
  173.7 129.0 %collective-permute-start.3 = (f32[1024,768]{1,0:T(8,128)}, f32[1024,768]{1,0:T(8,128)}, u32[]{:S(2)}, u32[]{:S(2)}) collective-permute-start(f32[1024,768]{1,0:T(8,128)} %back_rows.3), channel_id=1, source_target_pairs={{0,1},{1,0},{2,3},{3,2},{4,5},{5,4},{6,7},{7,6},{8,9},{9,8},{10,11... | collective-permute-start | bytes 9437192 | tf_op jit(solution)/shard_map/ppermute | solution.py:275
  178.8 6.0 %copy-start.20 = (u32[32]{0:T(128)S(1)}, u32[32]{0:T(128)}, u32[]{:S(2)}) copy-start(u32[32]{0:T(128)} %constant.28) | copy-start | bytes 388
  178.8 7.9 %copy-start.17 = (f32[384,1]{1,0:T(8,128)S(1)}, f32[384,1]{1,0:T(8,128)}, u32[]{:S(2)}) copy-start(f32[384,1]{1,0:T(8,128)} %get-tuple-element.48) | copy-start | bytes 4612
  178.8 7.9 %copy-start.18 = (f32[384,1]{1,0:T(8,128)S(1)}, f32[384,1]{1,0:T(8,128)}, u32[]{:S(2)}) copy-start(f32[384,1]{1,0:T(8,128)} %get-tuple-element.50) | copy-start | bytes 4612
  178.8 191.4 %collective-permute-start.1 = (f32[1024,768]{1,0:T(8,128)}, f32[1024,768]{1,0:T(8,128)}, u32[]{:S(2)}, u32[]{:S(2)}) collective-permute-start(f32[1024,768]{1,0:T(8,128)} %out_rows.3), channel_id=1, source_target_pairs={{0,1},{1,0},{2,3},{3,2},{4,5},{5,4},{6,7},{7,6},{8,9},{9,8},{10,11... | collective-permute-start | bytes 9437192 | tf_op jit(solution)/shard_map/ppermute | solution.py:277
  184.6 257.9 %collective-permute-start = (f32[1024,768]{1,0:T(8,128)S(1)}, f32[1024,768]{1,0:T(8,128)}, u32[]{:S(2)}, u32[]{:S(2)}) collective-permute-start(f32[1024,768]{1,0:T(8,128)S(1)} %out_rows.2), channel_id=1, source_target_pairs={{0,1},{1,0},{2,3},{3,2},{4,5},{5,4},{6,7},{7,6},{8,9},{9,8},{10,11... | collective-permute-start | bytes 9437192 | tf_op jit(solution)/shard_map/ppermute | solution.py:277
  188.1 3.0 copy-start.14
  188.1 182.1 %copy-start.19 = (f32[768]{0:T(1024)S(1)}, f32[768]{0:T(1024)}, u32[]{:S(2)}) copy-start(f32[768]{0:T(1024)} %param.12) | copy-start | bytes 9220
  449.5 1.9 copy-start.15
Sparse Core Ops, SparseCore 0:
  125.5 78.2 reduce-scatter.4
  208.4 110.4 reduce-scatter.6
